TPU v7x, 128 devices: a whole 4x4x4 slice. The times are simulated.
128 devices in a mesh: row: 8 (over z, core), col: 4 (over y), depth: 4 (over x).
Axes of the slice: x: 4, y: 4, z: 4, core: 2. Of those that a mesh axis runs over, the one named last changes fastest.
Arguments:
- traces: bfloat16 [32768, 16384], P(('col', 'depth'), 'row'), may hold values from -0.03125 to 0.03125
- features: bfloat16 [32768, 2048], P(('col', 'depth'), 'row'), may hold values from -6 to 6
- next_features: bfloat16 [32768, 2048], P(('col', 'depth'), 'row'), may hold values from -6 to 6
Outputs:
- panels: float32 [16384, 2048], P('row', ('col', 'depth'))
All inputs are finite; a program needn't handle non-finite values.
Results may differ from a plain program's by a relative error of at most 0.0028.
Values may be sent and summed in bfloat16 or wider, within the bound.
A program may use at most 128 MiB of HBM per device.

v0:
```python
import jax
import jax.numpy as jnp
from jax import lax
from jax.sharding import PartitionSpec as P

DISCOUNT = 0.99


def outer_sum(left, right):
    return lax.dot_general(
        left, right, (((0,), (0,)), ((), ())), preferred_element_type=jnp.float32
    )


def shards(traces, features, next_features):
    differences = (
        features.astype(jnp.float32) - DISCOUNT * next_features.astype(jnp.float32)
    ).astype(jnp.bfloat16)
    partial_sum = outer_sum(traces, lax.all_gather(differences, "row", axis=1, tiled=True))
    return lax.psum_scatter(partial_sum, ("col", "depth"), scatter_dimension=1, tiled=True)


def solution(mesh):
    return jax.shard_map(
        shards,
        mesh=mesh,
        in_specs=(
            P(("col", "depth"), "row"),
            P(("col", "depth"), "row"),
            P(("col", "depth"), "row"),
        ),
        out_specs=P("row", ("col", "depth")),
        check_vma=False,
    )
```

profile of v0, /device:TPU:16, one launch (start us, length us, event | category | flops | bytes accessed | tf_op | source)
XLA Modules:
  0.0 210.2 jit_solution(16848874493021881996)
XLA Ops:
  6.5 0.0 all-gather.2.cloned.1.call-start
  6.5 2.8 %subtract_convert_fusion = bf16[2048,256]{1,0:T(8,128)(2,1)} fusion(bf16[2048,256]{1,0:T(8,128)(2,1)} %param.5, bf16[2048,256]{1,0:T(8,128)(2,1)} %param.4), kind=kLoop, calls=%fused_computation.1 | loop fusion | flops 2621440 | bytes 3145728 | tf_op jit(solution)/shard_map/convert_element_type | solution.py:18
  9.4 0.0 all-gather.2.cloned.1.call-update
  9.4 0.0 reduce-scatter.2.cloned.1.call-start
  9.4 55.8 %all-gather.2.cloned.1.call-done = bf16[2048,2048]{1,0:T(8,128)(2,1)} async-done(((bf16[2048,256]{1,0:T(8,128)(2,1)}), bf16[2048,2048]{1,0:T(8,128)(2,1)}) %all-gather.2.cloned.1.call-update) | async-done | bytes 8388624 | tf_op jit(solution)/shard_map/all_gather | solution.py:19
  65.3 24.3 %convolution_bitcast_fusion = f32[2048,2048]{0,1:T(8,128)} fusion(bf16[2048,2048]{1,0:T(8,128)(2,1)} %all-gather.2.cloned.1.call-done, bf16[2048,2048]{1,0:T(8,128)(2,1)} %param.3), kind=kOutput, calls=%fused_computation | convolution fusion | flops 17179869184 | bytes 33554432 | tf_op jit(solution)/shard_map/dot_general | solution.py:10
  89.6 0.0 reduce-scatter.2.cloned.1.call-update
  89.6 111.3 %reduce-scatter.2.cloned.1.call-done = f32[2048,128]{0,1:T(8,128)} async-done(((f32[2048,2048]{0,1:T(8,128)}), f32[2048,128]{0,1:T(8,128)}) %reduce-scatter.2.cloned.1.call-update) | async-done | bytes 1048592 | tf_op jit(solution)/shard_map/reduce_scatter | solution.py:20
  200.9 2.5 %copy.4 = f32[2048,128]{1,0:T(8,128)} copy(f32[2048,128]{0,1:T(8,128)} %reduce-scatter.2.cloned.1.call-done) | data formatting | bytes 2097152 | tf_op jit(solution)/shard_map/reduce_scatter | solution.py:20
Async XLA Ops:
  6.5 58.7 %all-gather.2.cloned.1.call-start = ((), (), s32[]{:S(2)}) async-start(), calls=%async_computation.1 | async-start | bytes 9437184 | tf_op jit(solution)/shard_map/all_gather | solution.py:19
  9.4 191.5 %reduce-scatter.2.cloned.1.call-start = ((), (), s32[]{:S(2)}) async-start(), calls=%async_computation.2 | async-start | bytes 17825792 | tf_op jit(solution)/shard_map/reduce_scatter | solution.py:20
Sparse Core Ops, SparseCore 0:
  9.5 55.7 all-gather.1
  89.7 111.1 reduce-scatter.1
where the time goes:
time: 211 us; the launch traced here: 210 us
  waiting for transfers between devices  167 us (79%)
  matrix products  24.3 us (12%)
  between operations  13.4 us (6%)
  other arithmetic  2.83 us (1%)
  local copies, waits for them, and re-layouts  2.53 us (1%)
    reduce_scatter x1, waiting for transfers between devices, shards(): lax.psum_scatter(partial_sum, ('col', 'depth'), scatter_dimension=1, tile...  111 us
    all_gather x1, waiting for transfers between devices, shards(): lax.all_gather(differences, 'row', axis=1, tiled=True)  55.8 us
    dot_general x1, matrix products, outer_sum(): lax.dot_general(left, right, (((0,), (0,)), ((), ())), preferred_element_...  24.3 us
  transfers between devices with their start and end apart: 2, of which 2 were waited for; matrix products, arithmetic and copies ran while one was open for 0% of the time, Pallas kernels for 0%

commit v1 on v0

v1 whole, which is shorter than its diff:
```python
import jax
import jax.numpy as jnp
from jax import lax
from jax.experimental import pallas as pl
from jax.experimental.pallas import tpu as pltpu
from jax.sharding import PartitionSpec as P

DISCOUNT = 0.99
MESH = pl.DeviceIdType.MESH
F32, BF16 = jnp.float32, jnp.bfloat16
TILE = 256
UNIT = 16

UNITS = [2, 2, 2, 2]
AHEAD = 2
BATCHES = [
    [(0, 0), (0, 1)],
    [(0, 2), (0, 3)],
    [(1, 0), (3, 0)],
    [(1, 1), (3, 1)],
    [(2, 0), (2, 1)],
    [(1, 2), (3, 2)],
    [(1, 3), (3, 3)],
    [(2, 2), (2, 3)],
]
SPLIT = [1536, 1280, 1280, 1024, 1536, 768, 1024, 1536]
SCHEDULE = [
    "c0", "y10", "x10", "c1", "f0", "x11", "x20", "y20", "f1", "c2", "y12", "x12", "c3", "x13", "r0", "y22",
    "y13", "y30", "f2", "x21", "x23", "y23", "y32", "x22", "r1", "y11", "c5", "x15", "y15", "c4", "x14", "f3",
    "x31", "x32", "x33", "y14", "x30", "y40", "x25", "c6", "y16", "r2", "r3", "x24", "y25", "y21", "y24", "x16",
    "c7", "y17", "x17", "x26", "x34", "x41", "y33", "y50", "y34", "x40", "y27", "y26", "x27", "x44", "y44", "y35",
    "x36", "x35", "x51", "y43", "y31", "x37", "x42", "y36", "y45", "y41", "y37", "x47", "y46", "y42", "x43", "x54",
    "x46", "y54", "y55", "x45", "x53", "y47", "y57", "y53", "y56", "x56", "x55", "x57", "x50", "x52", "y51", "y52",
]

PIECES = len(UNITS)
FIRST = [sum(UNITS[:k]) for k in range(PIECES + 1)]
BASE = {}
for _groups in BATCHES:
    for _s, _k in _groups:
        BASE[_s, _k] = sum(4 * UNITS[k] for s, k in BASE)
CHUNK = {g: BASE[g] // 4 for g in BASE}
INDEX = {g: i for i, g in enumerate(BASE)}
ALL = FIRST[-1]
WX, WY = max(SPLIT), 2048 - min(SPLIT)


def kernel(
    traces, features, nexts, out,
    feat, nxt, weights, diff, p, pf, total,
    xda, xdb, xl, xr, xa, zd, za, zl, zr, wd, wa, wl, wr, vda, vdb, vl, vr, va,
    load, load_t, part, ring, ring_a, ring_b, ag_send,
    s_xda, s_xdb, s_xl, s_xr, s_x, s_zd, s_zl, s_zr, s_z, s_wd, s_wl, s_wr, s_w,
    s_vda, s_vdb, s_vl, s_vr, s_v,
):
    r, y, x = lax.axis_index("row"), lax.axis_index("col"), lax.axis_index("depth")
    z, h = r // 2, r % 2
    xp, xm, x2 = (x + 1) % 4, (x + 3) % 4, (x + 2) % 4
    east, west = {"depth": xp}, {"depth": xm}
    north, south = {"col": (y + 1) % 4}, {"col": (y + 3) % 4}
    up, down = {"row": (z + 1) % 4 * 2 + h}, {"row": (z + 3) % 4 * 2 + h}
    partner = {"row": z * 2 + 1 - h}
    tiles, rows = weights.shape[0], total.shape[-1]

    def send(src, dst, send_sem, recv_sem, where):
        pltpu.make_async_remote_copy(
            src_ref=src, dst_ref=dst, send_sem=send_sem, recv_sem=recv_sem, device_id=where, device_id_type=MESH
        ).start()

    def wait(ref, sem):
        pltpu.make_async_copy(ref, ref, sem).wait()

    first = [pltpu.make_async_copy(features, feat, load.at[0]), pltpu.make_async_copy(nexts, nxt, load.at[1])]
    for copy in first:
        copy.start()
    barrier = pltpu.get_barrier_semaphore()
    for where in (east, west, north, south, up, down, partner):
        pl.semaphore_signal(barrier, inc=1, device_id=where, device_id_type=MESH)

    def weight(t):
        columns = pl.ds(pl.multiple_of(t * TILE, TILE), TILE)
        return pltpu.make_async_copy(traces.at[:, columns], weights.at[t], load_t.at[t])

    for copy in first:
        copy.wait()
    for t in range(tiles):
        weight(t).start()

    @pl.loop(0, feat.shape[0] // 128)
    def _(t):
        tokens = pl.ds(pl.multiple_of(t * 128, 128), 128)
        d = feat[tokens, :].astype(F32) - DISCOUNT * nxt[tokens, :].astype(F32)
        d = d.astype(BF16).T.reshape(2, ALL, UNIT, 128)
        for b in range(2):
            for k in range(PIECES):
                u = UNITS[k]
                diff[pl.ds(BASE[0, k] + (2 * h + b) * u, u), :, tokens] = d[b, FIRST[k] : FIRST[k] + u]

    pl.semaphore_wait(barrier, 7)


    def mine(g):
        u = UNITS[g[1]]
        return diff.at[pl.ds(BASE[g] + 2 * h * u, 2 * u)]

    def theirs(g):
        u = UNITS[g[1]]
        return diff.at[pl.ds(BASE[g] + 2 * (1 - h) * u, 2 * u)]

    def one(g, b):
        u = UNITS[g[1]]
        return diff.at[pl.ds(BASE[g] + (2 * h + b) * u, u)]

    def ring_out(k):
        if k >= PIECES:
            return
        send(mine((0, k)), mine((3, k)), ag_send.at[INDEX[0, k]], ring.at[INDEX[3, k]], up)
        send(mine((0, k)), mine((1, k)), ag_send.at[INDEX[0, k]], ring.at[INDEX[1, k]], down)

    def to_partner(g):
        send(mine(g), mine(g), ag_send.at[INDEX[g]], part.at[INDEX[g]], partner)

    def forward(k):
        below, above, far = (3, k), (1, k), (2, k)
        wait(mine(below), ring.at[INDEX[below]])
        send(one(below, 0), one(far, 0), ag_send.at[INDEX[below]], ring_a.at[k], up)
        wait(mine(above), ring.at[INDEX[above]])
        send(one(above, 1), one(far, 1), ag_send.at[INDEX[above]], ring_b.at[k], down)
        ring_out(k + AHEAD)
        to_partner(below)
        to_partner(above)

    def far_end(k):
        far = (2, k)
        wait(one(far, 0), ring_a.at[k])
        wait(one(far, 1), ring_b.at[k])
        to_partner(far)


    def chunk(ref, g, i, lo, hi):
        u = UNITS[g[1]]
        return ref.at[pl.ds(BASE[g] + i * u, u), :, lo:hi]

    def exchange(g, lo, mid, hi, at, j, da, db, left, right, sends, s_da, s_db, s_l, s_r):
        n = mid - lo
        send(chunk(p, g, x2, lo, mid), da.at[at, :, 0:n], sends.at[j], s_da.at[j], east)
        send(chunk(p, g, x2, mid, hi), db.at[at, :, 0:n], sends.at[j], s_db.at[j], west)
        send(chunk(p, g, xp, mid, hi), left.at[at, :, n : 2 * n], sends.at[j], s_l.at[j], east)
        send(chunk(p, g, xm, lo, mid), right.at[at, :, 0:n], sends.at[j], s_r.at[j], west)

    def pass_on(g, lo, mid, hi, at, j, da, db, left, right, acc, sends, s_da, s_db, s_l, s_r):
        n = mid - lo
        wait(da.at[at, :, 0:n], s_da.at[j])
        acc[at, :, 0:n] = (chunk(pf, g, xp, lo, mid)[...] + da[at, :, 0:n].astype(F32)).astype(BF16)
        send(acc.at[at, :, 0:n], left.at[at, :, 0:n], sends.at[j], s_l.at[j], east)
        wait(db.at[at, :, 0:n], s_db.at[j])
        acc[at, :, n : 2 * n] = (chunk(pf, g, xm, mid, hi)[...] + db[at, :, 0:n].astype(F32)).astype(BF16)
        send(acc.at[at, :, n : 2 * n], right.at[at, :, n : 2 * n], sends.at[j], s_r.at[j], west)

    def parts(g):
        u = UNITS[g[1]]
        return pl.ds(CHUNK[g], u), INDEX[g], pl.ds(FIRST[g[1]], u), g[1]

    def x1(g, w, dy):
        at, j, _, _ = parts(g)
        exchange(g, 0, w // 2, w, at, j, xda, xdb, xl, xr, s_x, s_xda, s_xdb, s_xl, s_xr)

    def x2_(g, w, dy):
        at, j, _, _ = parts(g)
        pass_on(g, 0, w // 2, w, at, j, xda, xdb, xl, xr, xa, s_x, s_xda, s_xdb, s_xl, s_xr)

    def x3(g, w, dy):
        at, j, to, k = parts(g)
        n = w // 2
        wait(xl.at[at, :, 0:w], s_xl.at[j])
        wait(xr.at[at, :, 0:w], s_xr.at[j])
        own = chunk(pf, g, x, 0, w)
        summed = own[...] + xl[at, :, 0:w].astype(F32) + xr[at, :, 0:w].astype(F32)

        @pl.when(dy == 0)
        def _():
            total[to, :, 0:w] = summed

        @pl.when(dy != 0)
        def _():
            own[...] = summed
            chunk(p, g, x, 0, w)[...] = summed.astype(BF16)

        a, b = chunk(p, g, x, 0, n), chunk(p, g, x, n, w)

        @pl.when(dy == 2)
        def _():
            send(a, zd.at[at, :, 0:n], s_z.at[j], s_zd.at[j], south)
            send(b, zd.at[at, :, 0:n], s_z.at[j], s_zd.at[j], north)

        @pl.when(dy == 1)
        def _():
            send(b, zr.at[to, :, n:w], s_z.at[j], s_zr.at[k], south)

        @pl.when(dy == 3)
        def _():
            send(a, zl.at[to, :, 0:n], s_z.at[j], s_zl.at[k], north)

    def x4(g, w, dy):
        at, j, to, k = parts(g)
        n = w // 2

        @pl.when(dy == 1)
        def _():
            wait(zd.at[at, :, 0:n], s_zd.at[j])
            za[at, :, 0:n] = (chunk(pf, g, x, 0, n)[...] + zd[at, :, 0:n].astype(F32)).astype(BF16)
            send(za.at[at, :, 0:n], zr.at[to, :, 0:n], s_z.at[j], s_zr.at[k], south)

        @pl.when(dy == 3)
        def _():
            wait(zd.at[at, :, 0:n], s_zd.at[j])
            za[at, :, 0:n] = (chunk(pf, g, x, n, w)[...] + zd[at, :, 0:n].astype(F32)).astype(BF16)
            send(za.at[at, :, 0:n], zl.at[to, :, n:w], s_z.at[j], s_zl.at[k], north)

    def x5(g, w, dy):
        _, _, to, k = parts(g)

        @pl.when(dy == 0)
        def _():
            wait(zl.at[to, :, 0:w], s_zl.at[k])
            wait(zr.at[to, :, 0:w], s_zr.at[k])
            total[to, :, 0:w] += zl[to, :, 0:w].astype(F32) + zr[to, :, 0:w].astype(F32)

    def wide(g):
        u = UNITS[g[1]]
        return pl.ds(2 * CHUNK[g], 2 * u), 4 * FIRST[g[1]], 2 * u, BASE[g]

    def y1(g, w, dy):
        at, to, u, base = wide(g)
        _, j, _, k = parts(g)
        n = rows - w
        a, b = p.at[base : base + u, :, w:rows], p.at[base + u : base + 2 * u, :, w:rows]

        @pl.when(dy == 2)
        def _():
            send(a, wd.at[at, :, 0:n], s_w.at[j], s_wd.at[j], south)
            send(b, wd.at[at, :, 0:n], s_w.at[j], s_wd.at[j], north)

        @pl.when(dy == 1)
        def _():
            send(b, wr.at[to + u : to + 2 * u, :, 0:n], s_w.at[j], s_wr.at[k], south)

        @pl.when(dy == 3)
        def _():
            send(a, wl.at[to : to + u, :, 0:n], s_w.at[j], s_wl.at[k], north)

    def y2(g, w, dy):
        at, to, u, base = wide(g)
        _, j, _, k = parts(g)
        n = rows - w

        @pl.when(dy == 1)
        def _():
            wait(wd.at[at, :, 0:n], s_wd.at[j])
            wa[at, :, 0:n] = (pf[base : base + u, :, w:rows] + wd[at, :, 0:n].astype(F32)).astype(BF16)
            send(wa.at[at, :, 0:n], wr.at[to : to + u, :, 0:n], s_w.at[j], s_wr.at[k], south)

        @pl.when(dy == 3)
        def _():
            wait(wd.at[at, :, 0:n], s_wd.at[j])
            wa[at, :, 0:n] = (pf[base + u : base + 2 * u, :, w:rows] + wd[at, :, 0:n].astype(F32)).astype(BF16)
            send(wa.at[at, :, 0:n], wl.at[to + u : to + 2 * u, :, 0:n], s_w.at[j], s_wl.at[k], north)

    def y3(g, w, dy):
        _, to, u, base = wide(g)
        at, j, to1, k = parts(g)
        n = rows - w

        @pl.when(dy == 0)
        def _():
            wait(wl.at[to : to + 2 * u, :, 0:n], s_wl.at[k])
            wait(wr.at[to : to + 2 * u, :, 0:n], s_wr.at[k])

            @pl.loop(0, 2 * u)
            def _(i):
                summed = pf[base + i, :, w:rows] + wl[to + i, :, 0:n].astype(F32) + wr[to + i, :, 0:n].astype(F32)
                pf[base + i, :, w:rows] = summed
                p[base + i, :, w:rows] = summed.astype(BF16)

            exchange(g, w, (w + rows) // 2, rows, to1, k, vda, vdb, vl, vr, s_v, s_vda, s_vdb, s_vl, s_vr)

    def y4(g, w, dy):
        _, _, to, k = parts(g)

        @pl.when(dy == 0)
        def _():
            pass_on(g, w, (w + rows) // 2, rows, to, k, vda, vdb, vl, vr, va, s_v, s_vda, s_vdb, s_vl, s_vr)

    def y5(g, w, dy):
        _, _, to, k = parts(g)
        n = rows - w

        @pl.when(dy == 0)
        def _():
            wait(vl.at[to, :, 0:n], s_vl.at[k])
            wait(vr.at[to, :, 0:n], s_vr.at[k])
            total[to, :, w:rows] = (
                chunk(pf, g, x, w, rows)[...] + vl[to, :, 0:n].astype(F32) + vr[to, :, 0:n].astype(F32)
            )

    stages = {"x1": x1, "x2": x2_, "x3": x3, "x4": x4, "x5": x5, "y1": y1, "y2": y2, "y3": y3, "y4": y4, "y5": y5}
    loaded = []

    def compute(batch):
        groups = BATCHES[batch]
        for g in groups:
            wait(theirs(g), part.at[INDEX[g]])
        start, count = BASE[groups[0]], sum(4 * UNITS[k] for _, k in groups)
        unloaded = not loaded
        loaded.append(batch)

        @pl.loop(0, tiles)
        def _(t):
            if unloaded:
                weight(t).wait()
            left = diff[start : start + count].reshape(count * UNIT, diff.shape[-1])
            product = jnp.dot(left, weights[t], preferred_element_type=F32).reshape(count, UNIT, TILE)
            columns = pl.ds(pl.multiple_of(t * TILE, TILE), TILE)
            pf[start : start + count, :, columns] = product
            p[start : start + count, :, columns] = product.astype(BF16)

    for k in range(PIECES):
        to_partner((0, k))
        if k < AHEAD:
            ring_out(k)

    for step in SCHEDULE:
        name, n = step[:-1], int(step[-1])
        if name == "f":
            forward(n)
        elif name == "r":
            far_end(n)
        elif name == "c":
            compute(n)
        else:
            for g in BATCHES[n]:
                stages[name](g, SPLIT[n], (y - z - g[0] + 8) % 4)

    @pl.loop(0, rows // 128)
    def _(t):
        columns = pl.ds(pl.multiple_of(t * 128, 128), 128)
        out[columns, :] = total[:, :, columns].reshape(128, 128).T

    for batch, groups in enumerate(BATCHES):
        w = SPLIT[batch]
        for s, k in groups:
            j, u = INDEX[s, k], UNITS[k]
            wait(diff.at[0 : (6, 3, 2, 3)[s] * u], ag_send.at[j])
            wait(p.at[0 : 3 * u, :, 0:w], s_x.at[j])

            @pl.when((y - z - s + 8) % 4 != 0)
            def _():
                wait(p.at[0:u, :, 0:w], s_z.at[j])
                wait(p.at[0 : 4 * u, :, w:rows], s_w.at[j])

            @pl.when((y - z - s + 8) % 4 == 0)
            def _():
                wait(p.at[0 : 3 * u, :, w:rows], s_v.at[k])


def shards(traces, features, nexts):
    tokens, rows = traces.shape
    groups = len(BASE)
    vmem, dma = pltpu.VMEM, pltpu.SemaphoreType.DMA
    of_groups, of_pieces = dma((groups,)), dma((PIECES,))
    scratch = [
        vmem(features.shape, BF16), vmem(features.shape, BF16),
        vmem((rows // TILE, tokens, TILE), BF16),
        vmem((16 * ALL, UNIT, tokens), BF16),
        vmem((16 * ALL, UNIT, rows), BF16), vmem((16 * ALL, UNIT, rows), F32),
        vmem((ALL, UNIT, rows), F32),
        vmem((4 * ALL, UNIT, WX // 2), BF16), vmem((4 * ALL, UNIT, WX // 2), BF16),
        vmem((4 * ALL, UNIT, WX), BF16), vmem((4 * ALL, UNIT, WX), BF16), vmem((4 * ALL, UNIT, WX), BF16),
        vmem((4 * ALL, UNIT, WX // 2), BF16), vmem((4 * ALL, UNIT, WX // 2), BF16),
        vmem((ALL, UNIT, WX), BF16), vmem((ALL, UNIT, WX), BF16),
        vmem((8 * ALL, UNIT, WY), BF16), vmem((8 * ALL, UNIT, WY), BF16),
        vmem((4 * ALL, UNIT, WY), BF16), vmem((4 * ALL, UNIT, WY), BF16),
        vmem((ALL, UNIT, WY // 2), BF16), vmem((ALL, UNIT, WY // 2), BF16),
        vmem((ALL, UNIT, WY), BF16), vmem((ALL, UNIT, WY), BF16), vmem((ALL, UNIT, WY), BF16),
        dma((2,)), dma((rows // TILE,)), of_groups, of_groups, of_pieces, of_pieces, of_groups,
        of_groups, of_groups, of_groups, of_groups, of_groups,
        of_groups, of_pieces, of_pieces, of_groups,
        of_groups, of_pieces, of_pieces, of_groups,
        of_pieces, of_pieces, of_pieces, of_pieces, of_pieces,
    ]
    return pl.pallas_call(
        kernel,
        out_shape=jax.ShapeDtypeStruct((rows, features.shape[1] // 2), F32),
        in_specs=[pl.BlockSpec(memory_space=pl.ANY)] * 3,
        out_specs=pl.BlockSpec(memory_space=pltpu.VMEM),
        scratch_shapes=scratch,
        compiler_params=pltpu.CompilerParams(
            collective_id=0, has_side_effects=True, vmem_limit_bytes=67043328
        ),
        name="panels",
    )(traces, features, nexts)


def solution(mesh):
    return jax.shard_map(
        shards,
        mesh=mesh,
        in_specs=(P(("col", "depth"), "row"), P(("col", "depth"), "row"), P(("col", "depth"), "row")),
        out_specs=P("row", ("col", "depth")),
        check_vma=False,
    )
```

time: 211 us -> 77.9 us (0.37)
  waiting for transfers between devices: 167 us -> 0 us
  Pallas kernels: 0 us -> 74.4 us
  matrix products: 24.3 us -> 0 us
  between operations: 13.4 us -> 0.01 us
  other arithmetic: 2.83 us -> 0 us
    reduce_scatter x1 -> x0, waiting for transfers between devices: 111 us -> none  [shards(): lax.psum_scatter(partial_sum, ('col', 'depth'), scatter_dimension=1, tile...]
    pallas_call x0 -> x1, Pallas kernels: none -> 74.4 us  [shards(): pl.pallas_call(kernel, out_shape=jax.ShapeDtypeStruct((rows, features.sha...]
    all_gather x1 -> x0, waiting for transfers between devices: 55.8 us -> none  [shards(): lax.all_gather(differences, 'row', axis=1, tiled=True)]
    dot_general x1 -> x0, matrix products: 24.3 us -> none  [outer_sum(): lax.dot_general(left, right, (((0,), (0,)), ((), ())), preferred_element_...]
    convert_element_type x1 -> x0, other arithmetic: 2.83 us -> none  [shards(): differences = (features.astype(jnp.float32) - DISCOUNT * next_features.as...]
    reduce_scatter x1 -> x0, local copies, waits for them, and re-layouts: 2.53 us -> none  [shards(): lax.psum_scatter(partial_sum, ('col', 'depth'), scatter_dimension=1, tile...]
    unnamed x0 -> x1, local copies, waits for them, and re-layouts: none -> 2.26 us
  transfers between devices with their start and end apart: 2 -> 0, of which waited for: 2 -> 0; matrix products, arithmetic and copies ran while one was open for 0% -> 0% of each run, Pallas kernels for 0% -> 0%
where the time goes in v1:
time: 77.9 us; the launch traced here: 76.7 us
  Pallas kernels  74.4 us (96%)
  local copies, waits for them, and re-layouts  2.26 us (3%)
    pallas_call x1, Pallas kernels, shards(): pl.pallas_call(kernel, out_shape=jax.ShapeDtypeStruct((rows, features.sha...  74.4 us
    unnamed x1, local copies, waits for them, and re-layouts  2.26 us

profile of v1, /device:TPU:16, one launch (start us, length us, event | category | flops | bytes accessed | tf_op | source)
XLA Modules:
  0.0 76.7 jit_solution(14439827207516297060)
XLA Ops:
  0.0 74.4 %panels.1 = f32[2048,128]{1,0:T(8,128)} custom-call(bf16[2048,2048]{1,0:T(8,128)(2,1)} %traces.1, bf16[2048,256]{1,0:T(8,128)(2,1)} %features.1, bf16[2048,256]{1,0:T(8,128)(2,1)} %nexts.1), custom_call_target="tpu_custom_call" | custom-call | tf_op jit(solution)/shard_map/panels/pallas_call | solution.py:391
  74.4 2.3 %copy.5 = f32[2048,128]{1,0:T(8,128)} copy(f32[2048,128]{1,0:T(8,128)} %panels.1) | data formatting | bytes 2097152

commit v2 on v1

--- a/solution.py
+++ b/solution.py
@@ -8,7 +8,8 @@
 DISCOUNT = 0.99
 MESH = pl.DeviceIdType.MESH
 F32, BF16 = jnp.float32, jnp.bfloat16
-TILE = 256
+TILE = 1024
+CHUNKS = 4
 UNIT = 16
 
 UNITS = [2, 2, 2, 2]
@@ -18,19 +19,24 @@
     [(0, 2), (0, 3)],
     [(1, 0), (3, 0)],
     [(1, 1), (3, 1)],
-    [(2, 0), (2, 1)],
+    [(2, 0)],
     [(1, 2), (3, 2)],
+    [(2, 1)],
     [(1, 3), (3, 3)],
-    [(2, 2), (2, 3)],
+    [(2, 2)],
+    [(2, 3)],
 ]
-SPLIT = [1536, 1280, 1280, 1024, 1536, 768, 1024, 1536]
+SPLIT = [1024, 1280, 1024, 1024, 1280, 1536, 1536, 1024, 1536, 1280]
 SCHEDULE = [
-    "c0", "y10", "x10", "c1", "f0", "x11", "x20", "y20", "f1", "c2", "y12", "x12", "c3", "x13", "r0", "y22",
-    "y13", "y30", "f2", "x21", "x23", "y23", "y32", "x22", "r1", "y11", "c5", "x15", "y15", "c4", "x14", "f3",
-    "x31", "x32", "x33", "y14", "x30", "y40", "x25", "c6", "y16", "r2", "r3", "x24", "y25", "y21", "y24", "x16",
-    "c7", "y17", "x17", "x26", "x34", "x41", "y33", "y50", "y34", "x40", "y27", "y26", "x27", "x44", "y44", "y35",
-    "x36", "x35", "x51", "y43", "y31", "x37", "x42", "y36", "y45", "y41", "y37", "x47", "y46", "y42", "x43", "x54",
-    "x46", "y54", "y55", "x45", "x53", "y47", "y57", "y53", "y56", "x56", "x55", "x57", "x50", "x52", "y51", "y52",
+    "c.0", "y1.0", "x1.0", "c.1", "y1.1", "x1.1", "f.0", "x2.0", "c.2", "y1.2", "f.1", "x2.1", "x1.2", "c.3",
+    "y1.3", "x1.3", "r.0", "c.4", "x1.4", "y1.4", "x2.2", "f.2", "y2.1", "x2.3", "y2.2", "x2.4", "c.5", "y1.5",
+    "x1.5", "r.1", "y2.4", "x3.3", "x3.4", "c.6", "x1.6", "y1.6", "f.3", "x3.0", "y2.3", "x2.5", "x3.2", "y2.6",
+    "c.7", "y1.7", "x1.7", "x4.0", "x4.3", "r.2", "x2.6", "r.3", "x3.1", "x4.4", "c.8", "x1.8", "y1.8", "c.9",
+    "y1.9", "y3.4", "y2.0", "y3.1", "x5.0", "y2.7", "y3.6", "y2.5", "x1.9", "y2.8", "x2.7", "x3.5", "y3.8", "x4.2",
+    "x5.4", "y2.9", "x4.1", "x3.6", "x2.8", "x2.9", "y3.0", "y3.2", "y3.3", "y3.9", "x3.8", "y4.4", "x3.9", "y3.5",
+    "x4.5", "x3.7", "y4.1", "y4.6", "y3.7", "x5.2", "y4.0", "y4.9", "y4.2", "x5.1", "y5.4", "x4.6", "y4.3", "y4.8",
+    "x5.3", "x4.7", "y5.8", "x4.8", "x5.6", "y5.1", "y5.0", "y4.7", "y5.9", "x5.8", "x4.9", "y4.5", "y5.3", "x5.5",
+    "y5.2", "y5.7", "x5.7", "y5.6", "y5.5", "x5.9",
 ]
 
 PIECES = len(UNITS)
@@ -46,8 +52,8 @@
 
 
 def kernel(
-    traces, features, nexts, out,
-    feat, nxt, weights, diff, p, pf, total,
+    traces, features, nexts, total,
+    feat, nxt, weights, diff, p, pf,
     xda, xdb, xl, xr, xa, zd, za, zl, zr, wd, wa, wl, wr, vda, vdb, vl, vr, va,
     load, load_t, part, ring, ring_a, ring_b, ag_send,
     s_xda, s_xdb, s_xl, s_xr, s_x, s_zd, s_zl, s_zr, s_z, s_wd, s_wl, s_wr, s_w,
@@ -70,9 +76,18 @@
     def wait(ref, sem):
         pltpu.make_async_copy(ref, ref, sem).wait()
 
-    first = [pltpu.make_async_copy(features, feat, load.at[0]), pltpu.make_async_copy(nexts, nxt, load.at[1])]
-    for copy in first:
-        copy.start()
+    tokens = feat.shape[0] // CHUNKS
+
+    def loads(c):
+        some = pl.ds(c * tokens, tokens)
+        return [
+            pltpu.make_async_copy(features.at[some], feat.at[some], load.at[c]),
+            pltpu.make_async_copy(nexts.at[some], nxt.at[some], load.at[CHUNKS + c]),
+        ]
+
+    for c in range(CHUNKS):
+        for copy in loads(c):
+            copy.start()
     barrier = pltpu.get_barrier_semaphore()
     for where in (east, west, north, south, up, down, partner):
         pl.semaphore_signal(barrier, inc=1, device_id=where, device_id_type=MESH)
@@ -81,20 +96,22 @@
         columns = pl.ds(pl.multiple_of(t * TILE, TILE), TILE)
         return pltpu.make_async_copy(traces.at[:, columns], weights.at[t], load_t.at[t])
 
-    for copy in first:
-        copy.wait()
-    for t in range(tiles):
-        weight(t).start()
-
-    @pl.loop(0, feat.shape[0] // 128)
-    def _(t):
-        tokens = pl.ds(pl.multiple_of(t * 128, 128), 128)
-        d = feat[tokens, :].astype(F32) - DISCOUNT * nxt[tokens, :].astype(F32)
-        d = d.astype(BF16).T.reshape(2, ALL, UNIT, 128)
-        for b in range(2):
-            for k in range(PIECES):
-                u = UNITS[k]
-                diff[pl.ds(BASE[0, k] + (2 * h + b) * u, u), :, tokens] = d[b, FIRST[k] : FIRST[k] + u]
+    for c in range(CHUNKS):
+        for copy in loads(c):
+            copy.wait()
+        if c == CHUNKS - 1:
+            for t in range(tiles):
+                weight(t).start()
+
+        @pl.loop(c * tokens // 128, (c + 1) * tokens // 128)
+        def _(t):
+            some = pl.ds(pl.multiple_of(t * 128, 128), 128)
+            d = feat[some, :].astype(F32) - DISCOUNT * nxt[some, :].astype(F32)
+            d = d.astype(BF16).T.reshape(2, ALL, UNIT, 128)
+            for b in range(2):
+                for k in range(PIECES):
+                    u = UNITS[k]
+                    diff[pl.ds(BASE[0, k] + (2 * h + b) * u, u), :, some] = d[b, FIRST[k] : FIRST[k] + u]
 
     pl.semaphore_wait(barrier, 7)
 
@@ -330,7 +347,7 @@
             ring_out(k)
 
     for step in SCHEDULE:
-        name, n = step[:-1], int(step[-1])
+        name, n = step.split(".")[0], int(step.split(".")[1])
         if name == "f":
             forward(n)
         elif name == "r":
@@ -340,11 +357,6 @@
         else:
             for g in BATCHES[n]:
                 stages[name](g, SPLIT[n], (y - z - g[0] + 8) % 4)
-
-    @pl.loop(0, rows // 128)
-    def _(t):
-        columns = pl.ds(pl.multiple_of(t * 128, 128), 128)
-        out[columns, :] = total[:, :, columns].reshape(128, 128).T
 
     for batch, groups in enumerate(BATCHES):
         w = SPLIT[batch]
@@ -373,7 +385,6 @@
         vmem((rows // TILE, tokens, TILE), BF16),
         vmem((16 * ALL, UNIT, tokens), BF16),
         vmem((16 * ALL, UNIT, rows), BF16), vmem((16 * ALL, UNIT, rows), F32),
-        vmem((ALL, UNIT, rows), F32),
         vmem((4 * ALL, UNIT, WX // 2), BF16), vmem((4 * ALL, UNIT, WX // 2), BF16),
         vmem((4 * ALL, UNIT, WX), BF16), vmem((4 * ALL, UNIT, WX), BF16), vmem((4 * ALL, UNIT, WX), BF16),
         vmem((4 * ALL, UNIT, WX // 2), BF16), vmem((4 * ALL, UNIT, WX // 2), BF16),
@@ -382,15 +393,15 @@
         vmem((4 * ALL, UNIT, WY), BF16), vmem((4 * ALL, UNIT, WY), BF16),
         vmem((ALL, UNIT, WY // 2), BF16), vmem((ALL, UNIT, WY // 2), BF16),
         vmem((ALL, UNIT, WY), BF16), vmem((ALL, UNIT, WY), BF16), vmem((ALL, UNIT, WY), BF16),
-        dma((2,)), dma((rows // TILE,)), of_groups, of_groups, of_pieces, of_pieces, of_groups,
+        dma((2 * CHUNKS,)), dma((rows // TILE,)), of_groups, of_groups, of_pieces, of_pieces, of_groups,
         of_groups, of_groups, of_groups, of_groups, of_groups,
         of_groups, of_pieces, of_pieces, of_groups,
         of_groups, of_pieces, of_pieces, of_groups,
         of_pieces, of_pieces, of_pieces, of_pieces, of_pieces,
     ]
-    return pl.pallas_call(
+    transposed = pl.pallas_call(
         kernel,
-        out_shape=jax.ShapeDtypeStruct((rows, features.shape[1] // 2), F32),
+        out_shape=jax.ShapeDtypeStruct((ALL, UNIT, rows), F32),
         in_specs=[pl.BlockSpec(memory_space=pl.ANY)] * 3,
         out_specs=pl.BlockSpec(memory_space=pltpu.VMEM),
         scratch_shapes=scratch,
@@ -399,6 +410,7 @@
         ),
         name="panels",
     )(traces, features, nexts)
+    return transposed.reshape(ALL * UNIT, rows).T
 
 
 def solution(mesh):

time: 77.9 us -> 71.6 us (0.919); the launches traced: 76.7 us -> 71.5 us
  Pallas kernels: 74.4 us -> 68.9 us
    pallas_call x1, Pallas kernels: 74.4 us -> 68.9 us  [shards(): pl.pallas_call(kernel, out_shape=jax.ShapeDtypeStruct((ALL, UNIT, rows),...]
    reshape x0 -> x1, local copies, waits for them, and re-layouts: none -> 2.53 us  [shards(): return transposed.reshape(ALL * UNIT, rows).T]
    unnamed x1 -> x0, local copies, waits for them, and re-layouts: 2.26 us -> none
where the time goes in v2:
time: 71.6 us; the launch traced here: 71.5 us
  Pallas kernels  68.9 us (96%)
  local copies, waits for them, and re-layouts  2.53 us (4%)
    pallas_call x1, Pallas kernels, shards(): pl.pallas_call(kernel, out_shape=jax.ShapeDtypeStruct((ALL, UNIT, rows),...  68.9 us
    reshape x1, local copies, waits for them, and re-layouts, shards(): return transposed.reshape(ALL * UNIT, rows).T  2.53 us

profile of v2, /device:TPU:16, one launch (start us, length us, event | category | flops | bytes accessed | tf_op | source)
XLA Modules:
  0.0 71.5 jit_solution(10854328671711566834)
XLA Ops:
  0.0 68.9 %panels.1 = f32[8,16,2048]{2,1,0:T(8,128)} custom-call(bf16[2048,2048]{1,0:T(8,128)(2,1)} %traces.1, bf16[2048,256]{1,0:T(8,128)(2,1)} %features.1, bf16[2048,256]{1,0:T(8,128)(2,1)} %nexts.1), custom_call_target="tpu_custom_call" | custom-call | tf_op jit(solution)/shard_map/panels/pallas_call | solution.py:402
  68.9 2.5 %copy.4 = f32[128,2048]{0,1:T(8,128)} copy(f32[128,2048]{1,0:T(8,128)} %bitcast.2) | data formatting | bytes 2097152 | tf_op jit(solution)/shard_map/reshape | solution.py:413

commit v3 on v2

--- a/solution.py
+++ b/solution.py
@@ -8,35 +8,47 @@
 DISCOUNT = 0.99
 MESH = pl.DeviceIdType.MESH
 F32, BF16 = jnp.float32, jnp.bfloat16
-TILE = 1024
+TILE = 512
 CHUNKS = 4
 UNIT = 16
 
 UNITS = [2, 2, 2, 2]
 AHEAD = 2
 BATCHES = [
-    [(0, 0), (0, 1)],
-    [(0, 2), (0, 3)],
-    [(1, 0), (3, 0)],
-    [(1, 1), (3, 1)],
+    [(0, 0)],
+    [(0, 1)],
+    [(0, 2)],
+    [(0, 3)],
+    [(1, 0)],
+    [(3, 0)],
+    [(1, 1)],
+    [(3, 1)],
     [(2, 0)],
-    [(1, 2), (3, 2)],
+    [(1, 2)],
+    [(3, 2)],
     [(2, 1)],
-    [(1, 3), (3, 3)],
+    [(1, 3)],
+    [(3, 3)],
     [(2, 2)],
     [(2, 3)],
 ]
-SPLIT = [1024, 1280, 1024, 1024, 1280, 1536, 1536, 1024, 1536, 1280]
+SPLIT = [1024, 1280, 1280, 1280, 1280, 1536, 1024, 1024, 1024, 1536, 1024, 1536, 1024, 1536, 1536, 1280]
 SCHEDULE = [
-    "c.0", "y1.0", "x1.0", "c.1", "y1.1", "x1.1", "f.0", "x2.0", "c.2", "y1.2", "f.1", "x2.1", "x1.2", "c.3",
-    "y1.3", "x1.3", "r.0", "c.4", "x1.4", "y1.4", "x2.2", "f.2", "y2.1", "x2.3", "y2.2", "x2.4", "c.5", "y1.5",
-    "x1.5", "r.1", "y2.4", "x3.3", "x3.4", "c.6", "x1.6", "y1.6", "f.3", "x3.0", "y2.3", "x2.5", "x3.2", "y2.6",
-    "c.7", "y1.7", "x1.7", "x4.0", "x4.3", "r.2", "x2.6", "r.3", "x3.1", "x4.4", "c.8", "x1.8", "y1.8", "c.9",
-    "y1.9", "y3.4", "y2.0", "y3.1", "x5.0", "y2.7", "y3.6", "y2.5", "x1.9", "y2.8", "x2.7", "x3.5", "y3.8", "x4.2",
-    "x5.4", "y2.9", "x4.1", "x3.6", "x2.8", "x2.9", "y3.0", "y3.2", "y3.3", "y3.9", "x3.8", "y4.4", "x3.9", "y3.5",
-    "x4.5", "x3.7", "y4.1", "y4.6", "y3.7", "x5.2", "y4.0", "y4.9", "y4.2", "x5.1", "y5.4", "x4.6", "y4.3", "y4.8",
-    "x5.3", "x4.7", "y5.8", "x4.8", "x5.6", "y5.1", "y5.0", "y4.7", "y5.9", "x5.8", "x4.9", "y4.5", "y5.3", "x5.5",
-    "y5.2", "y5.7", "x5.7", "y5.6", "y5.5", "x5.9",
+    "c.0", "x1.0", "c.1", "x1.1", "d.0", "d.2", "d.3", "y1.3", "x2.0", "c.3", "x2.1", "x1.3", "y1.2", "f.0",
+    "c.2", "x1.2", "y1.0", "d.1", "x3.1", "c.5", "x1.5", "c.4", "d.5", "f.1", "y1.1", "x1.4", "x2.2", "d.4",
+    "y1.4", "x2.5", "y1.5", "d.7", "y1.7", "r.0", "d.6", "y1.6", "x2.4", "c.6", "x1.6", "c.7", "x1.7", "d.8",
+    "y1.8", "y2.4", "c.8", "x1.8", "x2.6", "f.2", "y2.7", "x3.2", "x2.7", "x3.4", "x3.5", "y2.6", "y2.0", "x2.8",
+    "c.10", "x1.10", "r.1", "y2.8", "c.9", "x1.9", "d.10", "y1.10", "x3.6", "c.11", "x1.11", "d.11", "y1.11", "x4.2",
+    "x3.8", "x4.4", "x2.9", "x3.7", "f.3", "d.9", "y1.9", "y2.1", "x2.3", "x2.10", "x2.11", "y2.11", "y2.5", "x4.8",
+    "y2.10", "r.2", "c.13", "x1.13", "x3.9", "c.12", "d.14", "y1.14", "x1.12", "r.3", "y3.8", "d.12", "y1.12", "x3.10",
+    "c.14", "x1.14", "d.15", "y1.15", "d.13", "x2.13", "y1.13", "y2.3", "c.15", "x1.15", "y2.9", "y3.4", "y2.14", "x4.10",
+    "x5.8", "x2.14", "x4.1", "x2.12", "x3.11", "y3.1", "y2.15", "y2.12", "y2.13", "y2.2", "x2.15", "y3.7", "x3.13", "y3.0",
+    "y3.3", "x3.3", "y3.10", "y3.6", "y3.11", "x5.10", "x3.0", "x3.14", "x4.11", "y3.9", "x4.5", "y3.14", "x3.12", "y3.2",
+    "x5.4", "y3.15", "y3.5", "y4.4", "y3.12", "x3.15", "y4.7", "x4.9", "x4.13", "y4.8", "x4.7", "y4.1", "x5.2", "y3.13",
+    "x4.14", "y4.3", "x4.6", "y4.11", "x4.3", "y4.2", "y4.9", "x4.0", "y4.15", "y4.10", "y4.0", "y4.6", "x4.15", "y4.5",
+    "x4.12", "y4.14", "y4.12", "y5.9", "y5.4", "x5.6", "y5.6", "y4.13", "x5.9", "x5.11", "x5.14", "y5.11", "y5.7", "y5.8",
+    "x5.12", "y5.5", "x5.13", "x5.0", "y5.15", "y5.12", "y5.14", "x5.3", "y5.10", "y5.3", "x5.7", "y5.2", "y5.1", "x5.5",
+    "x5.15", "y5.13", "x5.1", "y5.0",
 ]
 
 PIECES = len(UNITS)
@@ -52,10 +64,10 @@
 
 
 def kernel(
-    traces, features, nexts, total,
-    feat, nxt, weights, diff, p, pf,
+    traces, features, nexts, out,
+    feat, nxt, weights, diff, p, pf, total,
     xda, xdb, xl, xr, xa, zd, za, zl, zr, wd, wa, wl, wr, vda, vdb, vl, vr, va,
-    load, load_t, part, ring, ring_a, ring_b, ag_send,
+    load, load_t, leave, part, ring, ring_a, ring_b, ag_send,
     s_xda, s_xdb, s_xl, s_xr, s_x, s_zd, s_zl, s_zr, s_z, s_wd, s_wl, s_wr, s_w,
     s_vda, s_vdb, s_vl, s_vr, s_v,
 ):
@@ -66,7 +78,8 @@
     north, south = {"col": (y + 1) % 4}, {"col": (y + 3) % 4}
     up, down = {"row": (z + 1) % 4 * 2 + h}, {"row": (z + 3) % 4 * 2 + h}
     partner = {"row": z * 2 + 1 - h}
-    tiles, rows = weights.shape[0], total.shape[-1]
+    rows = total.shape[-1]
+    tiles = rows // TILE
 
     def send(src, dst, send_sem, recv_sem, where):
         pltpu.make_async_remote_copy(
@@ -93,8 +106,8 @@
         pl.semaphore_signal(barrier, inc=1, device_id=where, device_id_type=MESH)
 
     def weight(t):
-        columns = pl.ds(pl.multiple_of(t * TILE, TILE), TILE)
-        return pltpu.make_async_copy(traces.at[:, columns], weights.at[t], load_t.at[t])
+        some = pl.ds(t * TILE, TILE)
+        return pltpu.make_async_copy(traces.at[:, some], weights.at[:, some], load_t.at[t])
 
     for c in range(CHUNKS):
         for copy in loads(c):
@@ -234,6 +247,10 @@
             za[at, :, 0:n] = (chunk(pf, g, x, n, w)[...] + zd[at, :, 0:n].astype(F32)).astype(BF16)
             send(za.at[at, :, 0:n], zl.at[to, :, n:w], s_z.at[j], s_zl.at[k], north)
 
+    def result(k, lo, hi, j):
+        to = pl.ds(FIRST[k], UNITS[k])
+        return pltpu.make_async_copy(total.at[to, :, lo:hi], out.at[to, :, lo:hi], leave.at[j])
+
     def x5(g, w, dy):
         _, _, to, k = parts(g)
 
@@ -242,6 +259,7 @@
             wait(zl.at[to, :, 0:w], s_zl.at[k])
             wait(zr.at[to, :, 0:w], s_zr.at[k])
             total[to, :, 0:w] += zl[to, :, 0:w].astype(F32) + zr[to, :, 0:w].astype(F32)
+            result(k, 0, w, 2 * k).start()
 
     def wide(g):
         u = UNITS[g[1]]
@@ -319,27 +337,27 @@
             total[to, :, w:rows] = (
                 chunk(pf, g, x, w, rows)[...] + vl[to, :, 0:n].astype(F32) + vr[to, :, 0:n].astype(F32)
             )
+            result(k, w, rows, 2 * k + 1).start()
 
     stages = {"x1": x1, "x2": x2_, "x3": x3, "x4": x4, "x5": x5, "y1": y1, "y2": y2, "y3": y3, "y4": y4, "y5": y5}
-    loaded = []
-
-    def compute(batch):
+    waited = set()
+
+    def once(what, waiting):
+        if what not in waited:
+            waited.add(what)
+            waiting()
+
+    def compute(batch, lo, hi):
         groups = BATCHES[batch]
         for g in groups:
-            wait(theirs(g), part.at[INDEX[g]])
+            once(g, lambda g=g: wait(theirs(g), part.at[INDEX[g]]))
+        for t in range(lo // TILE, -(-hi // TILE)):
+            once(t, lambda t=t: weight(t).wait())
         start, count = BASE[groups[0]], sum(4 * UNITS[k] for _, k in groups)
-        unloaded = not loaded
-        loaded.append(batch)
-
-        @pl.loop(0, tiles)
-        def _(t):
-            if unloaded:
-                weight(t).wait()
-            left = diff[start : start + count].reshape(count * UNIT, diff.shape[-1])
-            product = jnp.dot(left, weights[t], preferred_element_type=F32).reshape(count, UNIT, TILE)
-            columns = pl.ds(pl.multiple_of(t * TILE, TILE), TILE)
-            pf[start : start + count, :, columns] = product
-            p[start : start + count, :, columns] = product.astype(BF16)
+        left = diff[start : start + count].reshape(count * UNIT, diff.shape[-1])
+        product = jnp.dot(left, weights[:, lo:hi], preferred_element_type=F32).reshape(count, UNIT, hi - lo)
+        pf[start : start + count, :, lo:hi] = product
+        p[start : start + count, :, lo:hi] = product.astype(BF16)
 
     for k in range(PIECES):
         to_partner((0, k))
@@ -353,7 +371,9 @@
         elif name == "r":
             far_end(n)
         elif name == "c":
-            compute(n)
+            compute(n, 0, SPLIT[n])
+        elif name == "d":
+            compute(n, SPLIT[n], rows)
         else:
             for g in BATCHES[n]:
                 stages[name](g, SPLIT[n], (y - z - g[0] + 8) % 4)
@@ -373,6 +393,8 @@
             @pl.when((y - z - s + 8) % 4 == 0)
             def _():
                 wait(p.at[0 : 3 * u, :, w:rows], s_v.at[k])
+                result(k, 0, w, 2 * k).wait()
+                result(k, w, rows, 2 * k + 1).wait()
 
 
 def shards(traces, features, nexts):
@@ -382,9 +404,10 @@
     of_groups, of_pieces = dma((groups,)), dma((PIECES,))
     scratch = [
         vmem(features.shape, BF16), vmem(features.shape, BF16),
-        vmem((rows // TILE, tokens, TILE), BF16),
+        vmem(traces.shape, BF16),
         vmem((16 * ALL, UNIT, tokens), BF16),
         vmem((16 * ALL, UNIT, rows), BF16), vmem((16 * ALL, UNIT, rows), F32),
+        vmem((ALL, UNIT, rows), F32),
         vmem((4 * ALL, UNIT, WX // 2), BF16), vmem((4 * ALL, UNIT, WX // 2), BF16),
         vmem((4 * ALL, UNIT, WX), BF16), vmem((4 * ALL, UNIT, WX), BF16), vmem((4 * ALL, UNIT, WX), BF16),
         vmem((4 * ALL, UNIT, WX // 2), BF16), vmem((4 * ALL, UNIT, WX // 2), BF16),
@@ -393,7 +416,7 @@
         vmem((4 * ALL, UNIT, WY), BF16), vmem((4 * ALL, UNIT, WY), BF16),
         vmem((ALL, UNIT, WY // 2), BF16), vmem((ALL, UNIT, WY // 2), BF16),
         vmem((ALL, UNIT, WY), BF16), vmem((ALL, UNIT, WY), BF16), vmem((ALL, UNIT, WY), BF16),
-        dma((2 * CHUNKS,)), dma((rows // TILE,)), of_groups, of_groups, of_pieces, of_pieces, of_groups,
+        dma((2 * CHUNKS,)), dma((rows // TILE,)), dma((2 * PIECES,)), of_groups, of_groups, of_pieces, of_pieces, of_groups,
         of_groups, of_groups, of_groups, of_groups, of_groups,
         of_groups, of_pieces, of_pieces, of_groups,
         of_groups, of_pieces, of_pieces, of_groups,
@@ -403,7 +426,7 @@
         kernel,
         out_shape=jax.ShapeDtypeStruct((ALL, UNIT, rows), F32),
         in_specs=[pl.BlockSpec(memory_space=pl.ANY)] * 3,
-        out_specs=pl.BlockSpec(memory_space=pltpu.VMEM),
+        out_specs=pl.BlockSpec(memory_space=pl.ANY),
         scratch_shapes=scratch,
         compiler_params=pltpu.CompilerParams(
             collective_id=0, has_side_effects=True, vmem_limit_bytes=67043328

time: 71.6 us -> 69.6 us (0.972)
  Pallas kernels: 68.9 us -> 66.9 us
    pallas_call x1, Pallas kernels: 68.9 us -> 66.9 us  [shards(): pl.pallas_call(kernel, out_shape=jax.ShapeDtypeStruct((ALL, UNIT, rows),...]
where the time goes in v3:
time: 69.6 us; the launch traced here: 69.4 us
  Pallas kernels  66.9 us (96%)
  local copies, waits for them, and re-layouts  2.53 us (4%)
    pallas_call x1, Pallas kernels, shards(): pl.pallas_call(kernel, out_shape=jax.ShapeDtypeStruct((ALL, UNIT, rows),...  66.9 us
    reshape x1, local copies, waits for them, and re-layouts, shards(): return transposed.reshape(ALL * UNIT, rows).T  2.53 us

profile of v3, /device:TPU:16, one launch (start us, length us, event | category | flops | bytes accessed | tf_op | source)
XLA Modules:
  0.0 69.4 jit_solution(7055253708771332082)
XLA Ops:
  0.0 66.9 %panels.1 = f32[8,16,2048]{2,1,0:T(8,128)} custom-call(bf16[2048,2048]{1,0:T(8,128)(2,1)} %traces.1, bf16[2048,256]{1,0:T(8,128)(2,1)} %features.1, bf16[2048,256]{1,0:T(8,128)(2,1)} %nexts.1), custom_call_target="tpu_custom_call" | custom-call | tf_op jit(solution)/shard_map/panels/pallas_call | solution.py:425
  66.9 2.5 %copy.4 = f32[128,2048]{0,1:T(8,128)} copy(f32[128,2048]{1,0:T(8,128)} %bitcast.2) | data formatting | bytes 2097152 | tf_op jit(solution)/shard_map/reshape | solution.py:436

commit v4 on v3

--- a/solution.py
+++ b/solution.py
@@ -98,12 +98,12 @@
             pltpu.make_async_copy(nexts.at[some], nxt.at[some], load.at[CHUNKS + c]),
         ]
 
+    barrier = pltpu.get_barrier_semaphore()
+    for where in (east, west, north, south, up, down, partner):
+        pl.semaphore_signal(barrier, inc=1, device_id=where, device_id_type=MESH)
     for c in range(CHUNKS):
         for copy in loads(c):
             copy.start()
-    barrier = pltpu.get_barrier_semaphore()
-    for where in (east, west, north, south, up, down, partner):
-        pl.semaphore_signal(barrier, inc=1, device_id=where, device_id_type=MESH)
 
     def weight(t):
         some = pl.ds(t * TILE, TILE)

time: 69.6 us -> 69.5 us (level)
  no operation moved by 1% of the time
where the time goes in v4:
time: 69.5 us; the launch traced here: 69.4 us
  Pallas kernels  66.8 us (96%)
  local copies, waits for them, and re-layouts  2.53 us (4%)
    pallas_call x1, Pallas kernels, shards(): pl.pallas_call(kernel, out_shape=jax.ShapeDtypeStruct((ALL, UNIT, rows),...  66.8 us
    reshape x1, local copies, waits for them, and re-layouts, shards(): return transposed.reshape(ALL * UNIT, rows).T  2.53 us

profile of v4, /device:TPU:16, one launch (start us, length us, event | category | flops | bytes accessed | tf_op | source)
XLA Modules:
  0.0 69.4 jit_solution(12541287048154737098)
XLA Ops:
  0.0 66.8 %panels.1 = f32[8,16,2048]{2,1,0:T(8,128)} custom-call(bf16[2048,2048]{1,0:T(8,128)(2,1)} %traces.1, bf16[2048,256]{1,0:T(8,128)(2,1)} %features.1, bf16[2048,256]{1,0:T(8,128)(2,1)} %nexts.1), custom_call_target="tpu_custom_call" | custom-call | tf_op jit(solution)/shard_map/panels/pallas_call | solution.py:425
  66.8 2.5 %copy.4 = f32[128,2048]{0,1:T(8,128)} copy(f32[128,2048]{1,0:T(8,128)} %bitcast.2) | data formatting | bytes 2097152 | tf_op jit(solution)/shard_map/reshape | solution.py:436
